TPU v7x, 32 devices: a whole 2x2x4 slice. The times are simulated.
32 devices in a mesh: shot: 4 (over x, core), tm: 8 (over z, y).
Axes of the slice: x: 2, y: 2, z: 4, core: 2. Of those that a mesh axis runs over, the one named last changes fastest.
Arguments:
- features: bfloat16 [8, 2048, 1024], P('shot', 'tm'), may hold values from -6 to 6
- weight_pool: bfloat16 [64, 128, 128], replicated, may hold values from -0.25 to 0.25
- pattern_in: int32 [24, 4], replicated, may hold values from 0 to 7
- pattern_pool: int32 [24, 4], replicated, may hold values from 0 to 63, as said below
- gate_weight: bfloat16 [1024, 16], replicated, may hold values from -0.1875 to 0.1875
- decay_rate: float32 [8], replicated, may hold values from 5e-05 to 0.04
- beta_bias: float32 [8], replicated, may hold values from -8 to -4
- norm_gain: float32 [128], replicated, may hold values from 0.25 to 1.75
- out_weight: bfloat16 [1024, 1024], replicated, may hold values from -0.1875 to 0.1875
- cotangent: bfloat16 [8, 2048, 1024], P('shot', 'tm'), may hold values from -6 to 6
Outputs:
- output: bfloat16 [8, 2048, 1024], P('shot', 'tm')
- weight_grad: bfloat16 [1024, 1024], replicated
- gain_grad: float32 [128], replicated
Inputs may be any that keep to these rules, and one draw needn't show every extreme that they name: `pattern_pool`: every weight block is used by some member.
All inputs are finite; a program needn't handle non-finite values.
Results may differ from a plain program's by a relative error of at most 0.0077.
Values sent between devices are 32-bit elements; how exact they have to be, the bound alone decides.
No kernel may reach another device: no remote copies, remote signals or barrier semaphores. Data moves between devices by JAX's collectives and lax.ppermute only.
A program may use at most 128 MiB of HBM per device.

v0:
```python
import math
import jax
import jax.numpy as jnp
from jax import lax
from jax.sharding import PartitionSpec as P

BLOCK = 64
FULL_PRECISION = lax.Precision.HIGHEST


def passed_along(block, axis, distance):
    devices = range(lax.axis_size(axis))
    route = [(i - distance, i) for i in devices if i - distance in devices]
    return lax.ppermute(block, axis, route)


def split_blocks(array, span):
    seqs, length = (array.shape[0], array.shape[1])
    shaped = array.reshape((seqs, length // span, span) + array.shape[2:])
    return jnp.moveaxis(shaped, 3, 2)


def multiply(left, right):
    return jnp.einsum("shcd,shde->shce", left, right, precision=FULL_PRECISION)


def chain_maps(earlier, later):
    return (multiply(later[0], earlier[0]), multiply(later[0], earlier[1]) + later[1])


def block_terms(queries, keys, values, logdecay, betas, span):
    query_h = split_blocks(queries, span)
    key_h = split_blocks(keys, span)
    value_h = split_blocks(values, span)
    beta_h = split_blocks(betas, span)
    cumulative = jnp.cumsum(split_blocks(logdecay, span), axis=-1)
    position = jnp.arange(span)
    strict = position[:, None] > position[None, :]
    inclusive = position[:, None] >= position[None, :]
    spread = cumulative[..., :, None] - cumulative[..., None, :]
    ratio_strict = jnp.where(strict, jnp.exp(jnp.where(strict, spread, 0.0)), 0.0)
    ratio_incl = jnp.where(inclusive, jnp.exp(jnp.where(inclusive, spread, 0.0)), 0.0)
    key_inner = jnp.einsum("snhtc,snhuc->snhtu", key_h, key_h, precision=FULL_PRECISION)
    system = jnp.eye(span, dtype=jnp.float32) + beta_h[..., :, None] * ratio_strict * key_inner
    growth = jnp.exp(cumulative)
    right_side = jnp.concatenate(
        [beta_h[..., None] * value_h, (beta_h * growth)[..., None] * key_h], axis=-1
    )
    solved = lax.linalg.triangular_solve(
        system, right_side, left_side=True, lower=True, unit_diagonal=True
    )
    value_width = value_h.shape[-1]
    pseudo = solved[..., :value_width]
    mixing = solved[..., value_width:]
    tail = jnp.exp(cumulative[..., -1:] - cumulative)
    weighted = key_h * tail[..., None]
    final = jnp.exp(cumulative[..., -1])
    identity = jnp.eye(key_h.shape[-1], dtype=jnp.float32)
    transit = final[..., None, None] * identity - jnp.einsum(
        "snhtc,snhtd->snhcd", weighted, mixing, precision=FULL_PRECISION
    )
    pushed = jnp.einsum("snhtc,snhtd->snhcd", weighted, pseudo, precision=FULL_PRECISION)
    attend = jnp.einsum("snhtc,snhuc->snhtu", query_h, key_h, precision=FULL_PRECISION) * ratio_incl
    return (query_h, growth, attend, pseudo, mixing, transit, pushed)


def shards(
    features,
    weight_pool,
    pattern_in,
    pattern_pool,
    gate_weight,
    decay_rate,
    beta_bias,
    norm_gain,
    out_weight,
    cotangent,
):
    seqs, length, width = features.shape
    heads = decay_rate.shape[0]
    dims = weight_pool.shape[1]
    count = seqs * length
    rows = features.reshape(count, width)
    blocks_in = rows.reshape(count, width // dims, dims)
    picked = jnp.take(blocks_in, pattern_in, axis=1)
    chosen = jnp.take(weight_pool, pattern_pool, axis=0)
    projected = jnp.einsum(
        "tojc,ojcd->tod", picked, chosen, preferred_element_type=jnp.float32
    ).astype(jnp.bfloat16)
    queries = projected[:, :heads].astype(jnp.float32)
    keys_raw = projected[:, heads : 2 * heads].astype(jnp.float32)
    keys = keys_raw * lax.rsqrt(jnp.sum(keys_raw * keys_raw, axis=-1, keepdims=True) + 1e-06)
    values = projected[:, 2 * heads :].astype(jnp.float32)
    gates = jnp.dot(rows, gate_weight, preferred_element_type=jnp.float32)
    logdecay = -decay_rate * jax.nn.softplus(gates[:, :heads])
    betas = jax.nn.sigmoid(gates[:, heads:] + beta_bias)
    terms = block_terms(
        queries.reshape(seqs, length, heads, dims),
        keys.reshape(seqs, length, heads, dims),
        values.reshape(seqs, length, heads, dims),
        logdecay.reshape(seqs, length, heads),
        betas.reshape(seqs, length, heads),
        BLOCK,
    )
    query_h, growth, attend, pseudo, mixing, transit, pushed = terms
    identity = jnp.broadcast_to(jnp.eye(dims, dtype=jnp.float32), (seqs, heads, dims, dims))
    empty = jnp.zeros((seqs, heads, dims, dims), jnp.float32)

    def compose(carry, item):
        return (chain_maps(carry, item), None)

    (total_map, total_push), _ = lax.scan(
        compose, (identity, empty), (jnp.moveaxis(transit, 1, 0), jnp.moveaxis(pushed, 1, 0))
    )

    def relay(turn, arriving):
        leaving = multiply(total_map, arriving) + total_push
        return passed_along(leaving, "tm", 1)

    incoming = lax.fori_loop(0, lax.axis_size("tm") - 1, relay, empty)

    def advance(state, item):
        query_n, growth_n, attend_n, pseudo_n, mixing_n, transit_n, pushed_n = item
        recalled = (
            jnp.einsum("shtc,shcd->shtd", query_n, state, precision=FULL_PRECISION)
            * growth_n[..., None]
        )
        corrected = pseudo_n - jnp.einsum(
            "shtc,shcd->shtd", mixing_n, state, precision=FULL_PRECISION
        )
        produced = recalled + jnp.einsum(
            "shtu,shud->shtd", attend_n, corrected, precision=FULL_PRECISION
        )
        return (multiply(transit_n, state) + pushed_n, produced)

    _, produced = lax.scan(advance, incoming, tuple((jnp.moveaxis(array, 1, 0) for array in terms)))
    core = jnp.transpose(produced, (1, 0, 3, 2, 4)).reshape(count, heads, dims)
    normal = core * lax.rsqrt(jnp.mean(core * core, axis=-1, keepdims=True) + 1e-05)
    mixed_in = (normal * norm_gain).astype(jnp.bfloat16).reshape(count, heads * dims)
    output = (
        jnp.dot(mixed_in, out_weight, preferred_element_type=jnp.float32)
        .astype(jnp.bfloat16)
        .reshape(seqs, length, width)
    )
    cot_rows = cotangent.reshape(count, width)
    back = lax.dot_general(
        cot_rows, out_weight, (((1,), (1,)), ((), ())), preferred_element_type=jnp.float32
    )
    gain_part = jnp.sum(back.reshape(count, heads, dims) * normal, axis=(0, 1))
    weight_part = lax.dot_general(
        mixed_in, cot_rows, (((0,), (0,)), ((), ())), preferred_element_type=jnp.float32
    )
    summed = lax.psum((weight_part, gain_part), ("shot", "tm"))
    scale = 1.0 / math.sqrt(count * lax.axis_size("shot") * lax.axis_size("tm"))
    weight_grad = (summed[0] * scale).astype(jnp.bfloat16)
    gain_grad = summed[1] * scale
    return (output, weight_grad, gain_grad)


def solution(mesh):
    placed = (P("shot", "tm", None), P(), P(), P(), P(), P(), P(), P(), P(), P("shot", "tm", None))
    return jax.shard_map(
        shards,
        mesh=mesh,
        in_specs=placed,
        out_specs=(P("shot", "tm", None), P(), P()),
        check_vma=False,
    )
```

profile of v0, /device:TPU:0, one launch (start us, length us, event | category | flops | bytes accessed | tf_op | source)
XLA Modules:
  0.0 862.9 jit_solution(17168145357962392265)
XLA Ops:
  12.1 4.3 gather_fusion
  16.4 4.7 copy.68
  21.3 6.8 gather_fusion.1
  28.1 11.5 %fusion.33 = bf16[512,24,128]{0,2,1:T(8,128)(2,1)} fusion(bf16[24,4,512,128]{3,2,1,0:T(8,128)(2,1)} %bitcast.199, pred[24,4]{1,0:T(8,128)(4,1)S(1)} %copy.69, bf16[24,4,128,128]{2,3,1,0:T(8,128)(2,1)} %copy.68, pred[24,4]{1,0:T(8,128)(4,1)S(1)} %copy.66), kind=kOutput, calls=%fused_computation.46 | convolution fusion | flops 1620049920 | bytes 18874560 | tf_op jit(solution)/shard_map/tojc,ojcd->tod/dot_general | solution.py:87
  56.5 7.6 add_bitcast_fusion
  64.1 316.0 %custom-call.3 = f32[2,4,8,1,64,64]{4,5,3,2,1,0:T(8,128)} custom-call(f32[2,4,8,1,64,64]{5,4,3,2,1,0:T(8,128)} %add_bitcast_fusion), custom_call_target="InvertDiagBlocksLowerTriangular" | custom-call | tf_op jit(solution)/shard_map/triangular_solve | solution.py:49
  383.7 3.8 fusion.29
  390.1 7.4 convolution_bitcast_fusion
  397.4 8.1 bitcast_subtract_fusion
  410.6 29.6 %while.37 = (s32[]{:T(128)}, f32[2,8,128,128]{3,2,1,0:T(8,128)S(1)}, f32[2,8,128,128]{3,2,1,0:T(8,128)}, f32[4,2,8,128,128]{4,3,2,1,0:T(8,128)}, f32[4,2,8,128,128]{4,3,2,1,0:T(8,128)}, /*index=5*/s32[]{:T(128)}, s32[]{:T(128)}) while((s32[]{:T(128)}, f32[2,8,128,128]{3,2,1,0:T(8,128)S(1)}, f32[2,8,128,128]{3,2,1,0:T(8,128)}, ...), condition=%wide.region_3.4_spmd.clone, body=%wide.region_2.3_spmd.clone.sunk | while | flops 805830656 | bytes 11535959 | solution.py:112
  450.0 200.3 %while.35 = (s32[]{:T(128)}, f32[2,8,128,128]{3,2,1,0:T(8,128)}, f32[2,8,128,128]{3,2,1,0:T(8,128)S(1)}, f32[2,8,128,128]{3,2,1,0:T(8,128)}, s32[]{:T(128)}) while((s32[]{:T(128)}, f32[2,8,128,128]{3,2,1,0:T(8,128)}, f32[2,8,128,128]{3,2,1,0:T(8,128)S(1)}, f32[2,8,128,128]{3,2,1,0:T(8,128)}, s32[]{:T(128)}) %tuple.68), condition=%wide.region_5.6_spmd, body=%wide.region_4.5_spmd.sunk | while | flops 402915328 | bytes 8388709 | solution.py:120
  453.6 5.9 collective-permute-start
  459.5 21.7 %collective-permute-done = f32[2,8,128,128]{3,2,1,0:T(8,128)} collective-permute-done((f32[2,8,128,128]{3,2,1,0:T(8,128)}, f32[2,8,128,128]{3,2,1,0:T(8,128)}, u32[]{:S(2)}, u32[]{:S(2)}) %collective-permute-start) | collective-permute-done | bytes 1048608 | tf_op jit(solution)/shard_map/while/body/eval_jaxpr/ppermute | solution.py:14
  484.9 5.4 collective-permute-start
  490.3 20.8 %collective-permute-done = f32[2,8,128,128]{3,2,1,0:T(8,128)} collective-permute-done((f32[2,8,128,128]{3,2,1,0:T(8,128)}, f32[2,8,128,128]{3,2,1,0:T(8,128)}, u32[]{:S(2)}, u32[]{:S(2)}) %collective-permute-start) | collective-permute-done | bytes 1048608 | tf_op jit(solution)/shard_map/while/body/eval_jaxpr/ppermute | solution.py:14
  514.8 5.4 collective-permute-start
  520.2 19.9 %collective-permute-done = f32[2,8,128,128]{3,2,1,0:T(8,128)} collective-permute-done((f32[2,8,128,128]{3,2,1,0:T(8,128)}, f32[2,8,128,128]{3,2,1,0:T(8,128)}, u32[]{:S(2)}, u32[]{:S(2)}) %collective-permute-start) | collective-permute-done | bytes 1048608 | tf_op jit(solution)/shard_map/while/body/eval_jaxpr/ppermute | solution.py:14
  543.8 6.3 collective-permute-start
  550.0 19.0 %collective-permute-done = f32[2,8,128,128]{3,2,1,0:T(8,128)} collective-permute-done((f32[2,8,128,128]{3,2,1,0:T(8,128)}, f32[2,8,128,128]{3,2,1,0:T(8,128)}, u32[]{:S(2)}, u32[]{:S(2)}) %collective-permute-start) | collective-permute-done | bytes 1048608 | tf_op jit(solution)/shard_map/while/body/eval_jaxpr/ppermute | solution.py:14
  572.6 6.3 collective-permute-start
  579.0 18.0 %collective-permute-done = f32[2,8,128,128]{3,2,1,0:T(8,128)} collective-permute-done((f32[2,8,128,128]{3,2,1,0:T(8,128)}, f32[2,8,128,128]{3,2,1,0:T(8,128)}, u32[]{:S(2)}, u32[]{:S(2)}) %collective-permute-start) | collective-permute-done | bytes 1048608 | tf_op jit(solution)/shard_map/while/body/eval_jaxpr/ppermute | solution.py:14
  600.7 6.3 collective-permute-start
  607.0 17.1 %collective-permute-done = f32[2,8,128,128]{3,2,1,0:T(8,128)} collective-permute-done((f32[2,8,128,128]{3,2,1,0:T(8,128)}, f32[2,8,128,128]{3,2,1,0:T(8,128)}, u32[]{:S(2)}, u32[]{:S(2)}) %collective-permute-start) | collective-permute-done | bytes 1048608 | tf_op jit(solution)/shard_map/while/body/eval_jaxpr/ppermute | solution.py:14
  627.8 6.3 collective-permute-start
  634.1 16.2 %collective-permute-done = f32[2,8,128,128]{3,2,1,0:T(8,128)} collective-permute-done((f32[2,8,128,128]{3,2,1,0:T(8,128)}, f32[2,8,128,128]{3,2,1,0:T(8,128)}, u32[]{:S(2)}, u32[]{:S(2)}) %collective-permute-start) | collective-permute-done | bytes 1048608 | tf_op jit(solution)/shard_map/while/body/eval_jaxpr/ppermute | solution.py:14
  650.3 48.3 %while.36 = (s32[]{:T(128)}, f32[2,8,128,128]{3,2,1,0:T(8,128)}, f32[4,2,8,64,128]{4,3,2,1,0:T(8,128)}, f32[4,2,8,128,128]{4,3,2,1,0:T(8,128)}, f32[4,2,8,128,12...) while((s32[]{:T(128)}, f32[2,8,128,128]{3,2,1,0:T(8,128)}, ...), condition=%wide.region_7.8_spmd, body=%wide.region_6.7_spmd.sunk | while | flops 906625024 | bytes 14171253 | solution.py:136
  658.6 3.8 convolution_add_fusion.7
  682.7 3.8 convolution_add_fusion.7
  719.4 43.5 %psum.15 = f32[128]{0:T(128)S(1)} all-reduce(f32[128]{0:T(128)S(1)} %fusion.44), channel_id=1, replica_groups=mesh['shot'=4,'tm'=8] {'shot','tm'}, use_global_device_ids=true, to_apply=%region_11.12 | all-reduce | flops 128 | bytes 1024 | tf_op jit(solution)/shard_map/psum | solution.py:153
  763.4 4.5 convolution_convert_fusion
  767.9 83.9 %all-reduce.2.cloned.1.call-done = f32[1024,1024]{1,0:T(8,128)} async-done(((f32[1024,1024]{1,0:T(8,128)}), f32[1024,1024]{1,0:T(8,128)}) %all-reduce.2.cloned.1.call-update) | async-done | bytes 4194320 | tf_op jit(solution)/shard_map/psum | solution.py:153
  851.8 4.1 multiply_convert_fusion
  (139 shorter events, 159.9 us)
Async XLA Ops:
  7.2 709.2 %copy-start = (bf16[1024,1024]{1,0:T(8,128)(2,1)S(1)}, bf16[1024,1024]{1,0:T(8,128)(2,1)}, u32[]{:S(2)}) copy-start(bf16[1024,1024]{1,0:T(8,128)(2,1)} %param.24) | copy-start | bytes 6291460
  7.2 844.6 %all-reduce.2.cloned.1.call-start = ((), (), s32[]{:S(2)}) async-start(), calls=%async_computation | async-start | bytes 8388608 | tf_op jit(solution)/shard_map/psum | solution.py:153
  41.1 3.8 copy-start.12
  41.1 3.8 copy-start.6
  41.1 3.8 copy-start.9
  41.1 4.2 copy-start.11
  380.1 3.6 copy-start.7
  387.5 2.6 copy-start.3
  442.6 2.8 copy-start.4
  442.6 2.8 copy-start.5
  453.6 27.6 %collective-permute-start = (f32[2,8,128,128]{3,2,1,0:T(8,128)}, f32[2,8,128,128]{3,2,1,0:T(8,128)}, u32[]{:S(2)}, u32[]{:S(2)}) collective-permute-start(f32[2,8,128,128]{3,2,1,0:T(8,128)} %convolution_add_fusion.6), channel_id=1, source_target_pairs={{0,1},{1,2},{2,3},{3,4},{4,5},{5,6},{6,7},{8,9},{9,10},{10,11},{11... | collective-permute-start | bytes 3145736 | tf_op jit(solution)/shard_map/while/body/eval_jaxpr/ppermute | solution.py:14
  484.9 26.2 %collective-permute-start = (f32[2,8,128,128]{3,2,1,0:T(8,128)}, f32[2,8,128,128]{3,2,1,0:T(8,128)}, u32[]{:S(2)}, u32[]{:S(2)}) collective-permute-start(f32[2,8,128,128]{3,2,1,0:T(8,128)} %convolution_add_fusion.6), channel_id=1, source_target_pairs={{0,1},{1,2},{2,3},{3,4},{4,5},{5,6},{6,7},{8,9},{9,10},{10,11},{11... | collective-permute-start | bytes 3145736 | tf_op jit(solution)/shard_map/while/body/eval_jaxpr/ppermute | solution.py:14
  514.8 25.3 %collective-permute-start = (f32[2,8,128,128]{3,2,1,0:T(8,128)}, f32[2,8,128,128]{3,2,1,0:T(8,128)}, u32[]{:S(2)}, u32[]{:S(2)}) collective-permute-start(f32[2,8,128,128]{3,2,1,0:T(8,128)} %convolution_add_fusion.6), channel_id=1, source_target_pairs={{0,1},{1,2},{2,3},{3,4},{4,5},{5,6},{6,7},{8,9},{9,10},{10,11},{11... | collective-permute-start | bytes 3145736 | tf_op jit(solution)/shard_map/while/body/eval_jaxpr/ppermute | solution.py:14
  543.8 25.2 %collective-permute-start = (f32[2,8,128,128]{3,2,1,0:T(8,128)}, f32[2,8,128,128]{3,2,1,0:T(8,128)}, u32[]{:S(2)}, u32[]{:S(2)}) collective-permute-start(f32[2,8,128,128]{3,2,1,0:T(8,128)} %convolution_add_fusion.6), channel_id=1, source_target_pairs={{0,1},{1,2},{2,3},{3,4},{4,5},{5,6},{6,7},{8,9},{9,10},{10,11},{11... | collective-permute-start | bytes 3145736 | tf_op jit(solution)/shard_map/while/body/eval_jaxpr/ppermute | solution.py:14
  572.6 24.3 %collective-permute-start = (f32[2,8,128,128]{3,2,1,0:T(8,128)}, f32[2,8,128,128]{3,2,1,0:T(8,128)}, u32[]{:S(2)}, u32[]{:S(2)}) collective-permute-start(f32[2,8,128,128]{3,2,1,0:T(8,128)} %convolution_add_fusion.6), channel_id=1, source_target_pairs={{0,1},{1,2},{2,3},{3,4},{4,5},{5,6},{6,7},{8,9},{9,10},{10,11},{11... | collective-permute-start | bytes 3145736 | tf_op jit(solution)/shard_map/while/body/eval_jaxpr/ppermute | solution.py:14
  600.7 23.4 %collective-permute-start = (f32[2,8,128,128]{3,2,1,0:T(8,128)}, f32[2,8,128,128]{3,2,1,0:T(8,128)}, u32[]{:S(2)}, u32[]{:S(2)}) collective-permute-start(f32[2,8,128,128]{3,2,1,0:T(8,128)} %convolution_add_fusion.6), channel_id=1, source_target_pairs={{0,1},{1,2},{2,3},{3,4},{4,5},{5,6},{6,7},{8,9},{9,10},{10,11},{11... | collective-permute-start | bytes 3145736 | tf_op jit(solution)/shard_map/while/body/eval_jaxpr/ppermute | solution.py:14
  627.8 22.5 %collective-permute-start = (f32[2,8,128,128]{3,2,1,0:T(8,128)}, f32[2,8,128,128]{3,2,1,0:T(8,128)}, u32[]{:S(2)}, u32[]{:S(2)}) collective-permute-start(f32[2,8,128,128]{3,2,1,0:T(8,128)} %convolution_add_fusion.6), channel_id=1, source_target_pairs={{0,1},{1,2},{2,3},{3,4},{4,5},{5,6},{6,7},{8,9},{9,10},{10,11},{11... | collective-permute-start | bytes 3145736 | tf_op jit(solution)/shard_map/while/body/eval_jaxpr/ppermute | solution.py:14
  698.5 2.4 copy-start.1
  698.6 2.4 copy-start.10
  700.9 1.4 copy-start.8
  705.7 3.4 copy-start.2
Sparse Core Ops, SparseCore 0:
  705.8 145.8 all-reduce.1
where the time goes:
time: 874 us; the launch traced here: 863 us
  other arithmetic  343 us (39%)
  waiting for transfers between devices  217 us (25%)
  matrix products  142 us (16%)
  local copies, waits for them, and re-layouts  61.3 us (7%)
  blocking collectives  43.5 us (5%)
  starting transfers between devices  42 us (5%)
  between operations  14.6 us (2%)
    another operation x2, other arithmetic, block_terms(): lax.linalg.triangular_solve(system, right_side, left_side=True, lower=Tru...  316 us
    ppermute x7, waiting for transfers between devices, passed_along(): return lax.ppermute(block, axis, route)  133 us
    psum x1, waiting for transfers between devices, shards(): summed = lax.psum((weight_part, gain_part), ('shot', 'tm'))  83.9 us
    dot_general x19, matrix products, multiply(): return jnp.einsum('shcd,shde->shce', left, right, precision=FULL_PRECISION)  65 us
    psum x1, blocking collectives, shards(): summed = lax.psum((weight_part, gain_part), ('shot', 'tm'))  43.5 us
    ppermute x7, starting transfers between devices, passed_along(): return lax.ppermute(block, axis, route)  42 us
  transfers between devices with their start and end apart: 8, of which 8 were waited for; matrix products, arithmetic and copies ran while one was open for 2% of the time, Pallas kernels for 0%

commit v1 on v0

--- a/solution.py
+++ b/solution.py
@@ -150,7 +150,7 @@
     weight_part = lax.dot_general(
         mixed_in, cot_rows, (((0,), (0,)), ((), ())), preferred_element_type=jnp.float32
     )
-    summed = lax.psum((weight_part, gain_part), ("shot", "tm"))
+    summed = lax.psum(lax.psum((weight_part, gain_part), "tm"), "shot")
     scale = 1.0 / math.sqrt(count * lax.axis_size("shot") * lax.axis_size("tm"))
     weight_grad = (summed[0] * scale).astype(jnp.bfloat16)
     gain_grad = summed[1] * scale

time: 874 us -> 975 us (1.12)
  waiting for transfers between devices: 217 us -> 336 us
  blocking collectives: 43.5 us -> 25.7 us
    psum x1 -> x2, waiting for transfers between devices: 83.9 us -> 203 us  [shards(): summed = lax.psum(lax.psum((weight_part, gain_part), 'tm'), 'shot')]
    psum x1 -> x2, blocking collectives: 43.5 us -> 25.7 us  [shards(): summed = lax.psum(lax.psum((weight_part, gain_part), 'tm'), 'shot')]
  transfers between devices with their start and end apart: 8 -> 9, of which waited for: 8 -> 9; matrix products, arithmetic and copies ran while one was open for 2% -> 2% of each run, Pallas kernels for 0% -> 0%
where the time goes in v1:
time: 975 us; the launch traced here: 964 us
  other arithmetic  343 us (35%)
  waiting for transfers between devices  336 us (34%)
  matrix products  142 us (15%)
  local copies, waits for them, and re-layouts  61.2 us (6%)
  starting transfers between devices  41.9 us (4%)
  blocking collectives  25.7 us (3%)
  between operations  14.6 us (1%)
    another operation x2, other arithmetic, block_terms(): lax.linalg.triangular_solve(system, right_side, left_side=True, lower=Tru...  316 us
    psum x2, waiting for transfers between devices, shards(): summed = lax.psum(lax.psum((weight_part, gain_part), 'tm'), 'shot')  203 us
    ppermute x7, waiting for transfers between devices, passed_along(): return lax.ppermute(block, axis, route)  133 us
    dot_general x19, matrix products, multiply(): return jnp.einsum('shcd,shde->shce', left, right, precision=FULL_PRECISION)  64.9 us
    ppermute x7, starting transfers between devices, passed_along(): return lax.ppermute(block, axis, route)  41.8 us
    psum x2, blocking collectives, shards(): summed = lax.psum(lax.psum((weight_part, gain_part), 'tm'), 'shot')  25.7 us
  transfers between devices with their start and end apart: 9, of which 9 were waited for; matrix products, arithmetic and copies ran while one was open for 2% of the time, Pallas kernels for 0%

profile of v1, /device:TPU:0, one launch (start us, length us, event | category | flops | bytes accessed | tf_op | source)
XLA Modules:
  0.0 964.1 jit_solution(536256946408133604)
XLA Ops:
  12.1 4.3 gather_fusion
  16.4 4.7 copy.68
  21.3 6.8 gather_fusion.1
  28.2 11.5 %fusion.33 = bf16[512,24,128]{0,2,1:T(8,128)(2,1)} fusion(bf16[24,4,512,128]{3,2,1,0:T(8,128)(2,1)} %bitcast.199, pred[24,4]{1,0:T(8,128)(4,1)S(1)} %copy.69, bf16[24,4,128,128]{2,3,1,0:T(8,128)(2,1)} %copy.68, pred[24,4]{1,0:T(8,128)(4,1)S(1)} %copy.66), kind=kOutput, calls=%fused_computation.46 | convolution fusion | flops 1620049920 | bytes 18874560 | tf_op jit(solution)/shard_map/tojc,ojcd->tod/dot_general | solution.py:87
  56.5 7.6 add_bitcast_fusion
  64.1 316.0 %custom-call.3 = f32[2,4,8,1,64,64]{4,5,3,2,1,0:T(8,128)} custom-call(f32[2,4,8,1,64,64]{5,4,3,2,1,0:T(8,128)} %add_bitcast_fusion), custom_call_target="InvertDiagBlocksLowerTriangular" | custom-call | tf_op jit(solution)/shard_map/triangular_solve | solution.py:49
  383.6 3.8 fusion.29
  390.0 7.4 convolution_bitcast_fusion
  397.3 8.1 bitcast_subtract_fusion
  410.5 29.6 %while.37 = (s32[]{:T(128)}, f32[2,8,128,128]{3,2,1,0:T(8,128)S(1)}, f32[2,8,128,128]{3,2,1,0:T(8,128)}, f32[4,2,8,128,128]{4,3,2,1,0:T(8,128)}, f32[4,2,8,128,128]{4,3,2,1,0:T(8,128)}, /*index=5*/s32[]{:T(128)}, s32[]{:T(128)}) while((s32[]{:T(128)}, f32[2,8,128,128]{3,2,1,0:T(8,128)S(1)}, f32[2,8,128,128]{3,2,1,0:T(8,128)}, ...), condition=%wide.region_3.4_spmd.clone, body=%wide.region_2.3_spmd.clone.sunk | while | flops 805830656 | bytes 11535959 | solution.py:112
  449.9 200.4 %while.35 = (s32[]{:T(128)}, f32[2,8,128,128]{3,2,1,0:T(8,128)}, f32[2,8,128,128]{3,2,1,0:T(8,128)S(1)}, f32[2,8,128,128]{3,2,1,0:T(8,128)}, s32[]{:T(128)}) while((s32[]{:T(128)}, f32[2,8,128,128]{3,2,1,0:T(8,128)}, f32[2,8,128,128]{3,2,1,0:T(8,128)S(1)}, f32[2,8,128,128]{3,2,1,0:T(8,128)}, s32[]{:T(128)}) %tuple.68), condition=%wide.region_5.6_spmd, body=%wide.region_4.5_spmd.sunk | while | flops 402915328 | bytes 8388709 | solution.py:120
  453.5 5.9 collective-permute-start
  459.4 21.7 %collective-permute-done = f32[2,8,128,128]{3,2,1,0:T(8,128)} collective-permute-done((f32[2,8,128,128]{3,2,1,0:T(8,128)}, f32[2,8,128,128]{3,2,1,0:T(8,128)}, u32[]{:S(2)}, u32[]{:S(2)}) %collective-permute-start) | collective-permute-done | bytes 1048608 | tf_op jit(solution)/shard_map/while/body/eval_jaxpr/ppermute | solution.py:14
  484.8 5.4 collective-permute-start
  490.2 20.8 %collective-permute-done = f32[2,8,128,128]{3,2,1,0:T(8,128)} collective-permute-done((f32[2,8,128,128]{3,2,1,0:T(8,128)}, f32[2,8,128,128]{3,2,1,0:T(8,128)}, u32[]{:S(2)}, u32[]{:S(2)}) %collective-permute-start) | collective-permute-done | bytes 1048608 | tf_op jit(solution)/shard_map/while/body/eval_jaxpr/ppermute | solution.py:14
  514.7 5.4 collective-permute-start
  520.1 19.9 %collective-permute-done = f32[2,8,128,128]{3,2,1,0:T(8,128)} collective-permute-done((f32[2,8,128,128]{3,2,1,0:T(8,128)}, f32[2,8,128,128]{3,2,1,0:T(8,128)}, u32[]{:S(2)}, u32[]{:S(2)}) %collective-permute-start) | collective-permute-done | bytes 1048608 | tf_op jit(solution)/shard_map/while/body/eval_jaxpr/ppermute | solution.py:14
  543.7 6.2 collective-permute-start
  549.9 19.0 %collective-permute-done = f32[2,8,128,128]{3,2,1,0:T(8,128)} collective-permute-done((f32[2,8,128,128]{3,2,1,0:T(8,128)}, f32[2,8,128,128]{3,2,1,0:T(8,128)}, u32[]{:S(2)}, u32[]{:S(2)}) %collective-permute-start) | collective-permute-done | bytes 1048608 | tf_op jit(solution)/shard_map/while/body/eval_jaxpr/ppermute | solution.py:14
  572.6 6.3 collective-permute-start
  578.8 18.1 %collective-permute-done = f32[2,8,128,128]{3,2,1,0:T(8,128)} collective-permute-done((f32[2,8,128,128]{3,2,1,0:T(8,128)}, f32[2,8,128,128]{3,2,1,0:T(8,128)}, u32[]{:S(2)}, u32[]{:S(2)}) %collective-permute-start) | collective-permute-done | bytes 1048608 | tf_op jit(solution)/shard_map/while/body/eval_jaxpr/ppermute | solution.py:14
  600.6 6.3 collective-permute-start
  606.9 17.1 %collective-permute-done = f32[2,8,128,128]{3,2,1,0:T(8,128)} collective-permute-done((f32[2,8,128,128]{3,2,1,0:T(8,128)}, f32[2,8,128,128]{3,2,1,0:T(8,128)}, u32[]{:S(2)}, u32[]{:S(2)}) %collective-permute-start) | collective-permute-done | bytes 1048608 | tf_op jit(solution)/shard_map/while/body/eval_jaxpr/ppermute | solution.py:14
  627.7 6.3 collective-permute-start
  634.0 16.2 %collective-permute-done = f32[2,8,128,128]{3,2,1,0:T(8,128)} collective-permute-done((f32[2,8,128,128]{3,2,1,0:T(8,128)}, f32[2,8,128,128]{3,2,1,0:T(8,128)}, u32[]{:S(2)}, u32[]{:S(2)}) %collective-permute-start) | collective-permute-done | bytes 1048608 | tf_op jit(solution)/shard_map/while/body/eval_jaxpr/ppermute | solution.py:14
  650.2 48.2 %while.36 = (s32[]{:T(128)}, f32[2,8,128,128]{3,2,1,0:T(8,128)}, f32[4,2,8,64,128]{4,3,2,1,0:T(8,128)}, f32[4,2,8,128,128]{4,3,2,1,0:T(8,128)}, f32[4,2,8,128,12...) while((s32[]{:T(128)}, f32[2,8,128,128]{3,2,1,0:T(8,128)}, ...), condition=%wide.region_7.8_spmd, body=%wide.region_6.7_spmd.sunk | while | flops 906625024 | bytes 14171253 | solution.py:136
  705.6 160.4 %all-reduce.3.cloned.1.call-done = f32[1024,1024]{1,0:T(8,128)} async-done(((f32[1024,1024]{1,0:T(8,128)}), f32[1024,1024]{1,0:T(8,128)}) %all-reduce.3.cloned.1.call-update) | async-done | bytes 4194320 | tf_op jit(solution)/shard_map/psum | solution.py:153
  879.6 19.1 %psum.30 = f32[128]{0:T(128)S(1)} all-reduce(f32[128]{0:T(128)S(1)} %fusion.44), channel_id=1, replica_groups=mesh['shot'=4,'tm'=8] {'tm'}, use_global_device_ids=true, to_apply=%region_12.13 | all-reduce | flops 128 | bytes 1024 | tf_op jit(solution)/shard_map/psum | solution.py:153
  898.8 6.5 psum.31
  905.8 4.5 convolution_convert_fusion
  910.4 42.6 %all-reduce.5.cloned.1.call-done = f32[1024,1024]{1,0:T(8,128)} async-done(((f32[1024,1024]{1,0:T(8,128)}), f32[1024,1024]{1,0:T(8,128)}) %all-reduce.5.cloned.1.call-update) | async-done | bytes 4194320 | tf_op jit(solution)/shard_map/psum | solution.py:153
  953.0 4.1 multiply_convert_fusion
  (143 shorter events, 167.2 us)
Async XLA Ops:
  7.2 869.4 %copy-start = (bf16[1024,1024]{1,0:T(8,128)(2,1)S(1)}, bf16[1024,1024]{1,0:T(8,128)(2,1)}, u32[]{:S(2)}) copy-start(bf16[1024,1024]{1,0:T(8,128)(2,1)} %param.24) | copy-start | bytes 6291460
  7.2 858.8 %all-reduce.3.cloned.1.call-start = ((), (), s32[]{:S(2)}) async-start(), calls=%async_computation | async-start | bytes 8388608 | tf_op jit(solution)/shard_map/psum | solution.py:153
  41.1 3.8 copy-start.12
  41.1 3.8 copy-start.6
  41.1 3.8 copy-start.9
  41.1 4.1 copy-start.11
  380.0 3.6 copy-start.7
  387.4 2.5 copy-start.3
  442.5 2.8 copy-start.4
  442.5 2.8 copy-start.5
  453.5 27.6 %collective-permute-start = (f32[2,8,128,128]{3,2,1,0:T(8,128)}, f32[2,8,128,128]{3,2,1,0:T(8,128)}, u32[]{:S(2)}, u32[]{:S(2)}) collective-permute-start(f32[2,8,128,128]{3,2,1,0:T(8,128)} %convolution_add_fusion.6), channel_id=1, source_target_pairs={{0,1},{1,2},{2,3},{3,4},{4,5},{5,6},{6,7},{8,9},{9,10},{10,11},{11... | collective-permute-start | bytes 3145736 | tf_op jit(solution)/shard_map/while/body/eval_jaxpr/ppermute | solution.py:14
  484.8 26.2 %collective-permute-start = (f32[2,8,128,128]{3,2,1,0:T(8,128)}, f32[2,8,128,128]{3,2,1,0:T(8,128)}, u32[]{:S(2)}, u32[]{:S(2)}) collective-permute-start(f32[2,8,128,128]{3,2,1,0:T(8,128)} %convolution_add_fusion.6), channel_id=1, source_target_pairs={{0,1},{1,2},{2,3},{3,4},{4,5},{5,6},{6,7},{8,9},{9,10},{10,11},{11... | collective-permute-start | bytes 3145736 | tf_op jit(solution)/shard_map/while/body/eval_jaxpr/ppermute | solution.py:14
  514.7 25.3 %collective-permute-start = (f32[2,8,128,128]{3,2,1,0:T(8,128)}, f32[2,8,128,128]{3,2,1,0:T(8,128)}, u32[]{:S(2)}, u32[]{:S(2)}) collective-permute-start(f32[2,8,128,128]{3,2,1,0:T(8,128)} %convolution_add_fusion.6), channel_id=1, source_target_pairs={{0,1},{1,2},{2,3},{3,4},{4,5},{5,6},{6,7},{8,9},{9,10},{10,11},{11... | collective-permute-start | bytes 3145736 | tf_op jit(solution)/shard_map/while/body/eval_jaxpr/ppermute | solution.py:14
  543.7 25.2 %collective-permute-start = (f32[2,8,128,128]{3,2,1,0:T(8,128)}, f32[2,8,128,128]{3,2,1,0:T(8,128)}, u32[]{:S(2)}, u32[]{:S(2)}) collective-permute-start(f32[2,8,128,128]{3,2,1,0:T(8,128)} %convolution_add_fusion.6), channel_id=1, source_target_pairs={{0,1},{1,2},{2,3},{3,4},{4,5},{5,6},{6,7},{8,9},{9,10},{10,11},{11... | collective-permute-start | bytes 3145736 | tf_op jit(solution)/shard_map/while/body/eval_jaxpr/ppermute | solution.py:14
  572.6 24.4 %collective-permute-start = (f32[2,8,128,128]{3,2,1,0:T(8,128)}, f32[2,8,128,128]{3,2,1,0:T(8,128)}, u32[]{:S(2)}, u32[]{:S(2)}) collective-permute-start(f32[2,8,128,128]{3,2,1,0:T(8,128)} %convolution_add_fusion.6), channel_id=1, source_target_pairs={{0,1},{1,2},{2,3},{3,4},{4,5},{5,6},{6,7},{8,9},{9,10},{10,11},{11... | collective-permute-start | bytes 3145736 | tf_op jit(solution)/shard_map/while/body/eval_jaxpr/ppermute | solution.py:14
  600.6 23.4 %collective-permute-start = (f32[2,8,128,128]{3,2,1,0:T(8,128)}, f32[2,8,128,128]{3,2,1,0:T(8,128)}, u32[]{:S(2)}, u32[]{:S(2)}) collective-permute-start(f32[2,8,128,128]{3,2,1,0:T(8,128)} %convolution_add_fusion.6), channel_id=1, source_target_pairs={{0,1},{1,2},{2,3},{3,4},{4,5},{5,6},{6,7},{8,9},{9,10},{10,11},{11... | collective-permute-start | bytes 3145736 | tf_op jit(solution)/shard_map/while/body/eval_jaxpr/ppermute | solution.py:14
  627.7 22.5 %collective-permute-start = (f32[2,8,128,128]{3,2,1,0:T(8,128)}, f32[2,8,128,128]{3,2,1,0:T(8,128)}, u32[]{:S(2)}, u32[]{:S(2)}) collective-permute-start(f32[2,8,128,128]{3,2,1,0:T(8,128)} %convolution_add_fusion.6), channel_id=1, source_target_pairs={{0,1},{1,2},{2,3},{3,4},{4,5},{5,6},{6,7},{8,9},{9,10},{10,11},{11... | collective-permute-start | bytes 3145736 | tf_op jit(solution)/shard_map/while/body/eval_jaxpr/ppermute | solution.py:14
  698.4 2.4 copy-start.1
  698.4 2.4 copy-start.10
  700.8 1.4 copy-start.8
  705.5 247.5 %all-reduce.5.cloned.1.call-start = ((), (), s32[]{:S(2)}) async-start(), calls=%async_computation.1 | async-start | bytes 8388608 | tf_op jit(solution)/shard_map/psum | solution.py:153
  866.0 3.4 copy-start.2
Sparse Core Ops, SparseCore 0:
  705.6 160.2 all-reduce.2
  868.3 84.6 all-reduce.4
